TPU v7x, 128 devices: a whole 4x4x4 slice. The times are simulated.
128 devices in a mesh: grp: 2 (over y_lo), tp: 64 (over y_hi, z, x, core).
Axes of the slice: x: 4, y: 4 (y_hi: 2, y_lo: 2; y = y_hi * 2 + y_lo), z: 4, core: 2. Of those that a mesh axis runs over, the one named last changes fastest.
Arguments:
- patches: bfloat16 [5120, 1408], P('tp'), may hold values from -6 to 6
- grids: int32 [64, 3, 2], P('tp'), may hold values from 0 to 40, as said below
- positions: int32 [1280], replicated, may hold values from 0 to 2048, as said below
- vis_gain: float32 [1408], replicated, may hold values from 0.1 to 1.9
- vis_query: bfloat16 [1408, 1408], P(None, 'grp')
- vis_key: bfloat16 [1408, 1408], P(None, 'grp'), may hold values from -0.15625 to 0.15625
- vis_value: bfloat16 [1408, 1408], P(None, 'grp'), may hold values from -0.15625 to 0.15625
- vis_out: bfloat16 [1408, 1408], P('grp'), may hold values from -0.15625 to 0.15625
- w_proj: bfloat16 [5632, 4096], P(None, 'tp'), may hold values from -0.078125 to 0.078125
- text_embed: bfloat16 [2048, 4096], P(('grp', 'tp')), may hold values from -6 to 6
- slots: int32 [2, 512], P('grp'), may hold values from 0 to 1023, as said below
- lengths: int32 [2, 8], P('grp'), may hold values from 1 to 256, 1024 in all within a row
- attn_gain: float32 [4096], replicated, may hold values from 0.1 to 1.9
- mlp_gain: float32 [4096], replicated, may hold values from 0.1 to 1.9
- w_kv: bfloat16 [4096, 8192], P(None, 'tp'), may hold values from -0.09375 to 0.09375
- w_gate: bfloat16 [4096, 11008], P(None, 'tp'), may hold values from -0.09375 to 0.09375
- w_up: bfloat16 [4096, 11008], P(None, 'tp'), may hold values from -0.09375 to 0.09375
- w_down: bfloat16 [11008, 4096], P('tp'), may hold values from -0.0546875 to 0.0546875
Outputs:
- layer_out: bfloat16 [2048, 4096], P(('grp', 'tp'))
- kv_out: bfloat16 [2, 512, 8192], P('grp', None, 'tp')
Inputs may be any that keep to these rules, and one draw needn't show every extreme that they name: `grids`: heights and widths are even; the areas of one tp index sum to at most 80; a height of 0 marks an empty entry. `positions`: every merged cell slot inside an image holds a distinct prompt position below 2048, increasing with the slot; slots past a block's images hold 2048. `slots`: distinct within each batch.
All inputs are finite; a program needn't handle non-finite values.
Results may differ from a plain program's by a relative error of at most 0.014.
The roundings to bfloat16 on the way count: a program that leaves them out, or rounds other values in their place, can miss the bound.
Values may be sent and summed in bfloat16 or wider, within the bound.
A program may use at most 128 MiB of HBM per device.

v0:
```python
import math

import jax
import jax.numpy as jnp
from jax import lax
from jax.sharding import PartitionSpec as P

VHD = 88
HD = 128
PATCH_DEV = 80
MERGE_DEV = 20
IMGS = 3


def layer_norm(row_data, gain_vec):
    as_float = row_data.astype(jnp.float32)
    center = as_float - jnp.mean(as_float, axis=-1, keepdims=True)
    spread = jnp.mean(center * center, axis=-1, keepdims=True)
    return (center * lax.rsqrt(spread + 1e-06) * gain_vec).astype(jnp.bfloat16)


def rms_norm(row_data, gain_vec):
    as_float = row_data.astype(jnp.float32)
    square_mean = jnp.mean(as_float * as_float, axis=-1, keepdims=True)
    return (as_float * lax.rsqrt(square_mean + 1e-05) * gain_vec).astype(jnp.bfloat16)


def image_tables(grid_dev):
    heights = grid_dev[:, 0]
    widths = grid_dev[:, 1]
    areas = heights * widths
    seg_ends = jnp.cumsum(areas)
    slot_ids = jnp.arange(PATCH_DEV, dtype=jnp.int32)
    segment = jnp.sum((slot_ids[:, None] >= seg_ends[None, :]).astype(jnp.int32), axis=1)
    cell_areas = areas // 4
    cell_ends = jnp.cumsum(cell_areas)
    cell_starts = cell_ends - cell_areas
    cell_ids = jnp.arange(MERGE_DEV, dtype=jnp.int32)
    which = jnp.sum((cell_ids[:, None] >= cell_ends[None, :]).astype(jnp.int32), axis=1)
    which = jnp.minimum(which, IMGS - 1)
    select = (which[:, None] == jnp.arange(IMGS, dtype=jnp.int32)[None, :]).astype(jnp.int32)
    start_cell = jnp.sum(select * cell_starts[None, :], axis=1)
    width_sel = jnp.sum(select * widths[None, :], axis=1)
    half_width = jnp.maximum(width_sel // 2, 1)
    inner = cell_ids - start_cell
    row_pair = inner // half_width
    col_pair = inner % half_width
    corner = 4 * start_cell + 2 * row_pair * width_sel + 2 * col_pair
    corners = jnp.stack([corner, corner + 1, corner + width_sel, corner + width_sel + 1], axis=1)
    valid = cell_ids < cell_ends[IMGS - 1]
    return (segment, jnp.where(valid[:, None], corners, 0))


def rotate_keys(values_f, token_pos, first_col):
    col_count = values_f.shape[1]
    col_ids = first_col + jnp.arange(0, col_count, 2, dtype=jnp.int32)
    pair_ids = col_ids % HD // 2
    is_key = col_ids // HD % 2 == 0
    freq = jnp.exp(pair_ids.astype(jnp.float32) * (-2.0 * math.log(10000.0) / HD))
    angle = token_pos.astype(jnp.float32)[:, None] * freq[None, :]
    cosine = jnp.where(is_key[None, :], jnp.cos(angle), 1.0)
    sine = jnp.where(is_key[None, :], jnp.sin(angle), 0.0)
    paired = values_f.reshape(values_f.shape[0], col_count // 2, 2)
    even_part = paired[:, :, 0]
    odd_part = paired[:, :, 1]
    turned = jnp.stack(
        [even_part * cosine - odd_part * sine, even_part * sine + odd_part * cosine], axis=2
    )
    return turned.reshape(values_f.shape[0], col_count)


def slot_positions(slot_ids, length_row):
    req_ends = jnp.cumsum(length_row)
    req_starts = req_ends - length_row
    inside = (slot_ids[:, None] >= req_starts[None, :]) & (slot_ids[:, None] < req_ends[None, :])
    return slot_ids - jnp.sum(jnp.where(inside, req_starts[None, :], 0), axis=1)


def local(
    patches,
    grids,
    positions,
    vis_gain,
    vis_query,
    vis_key,
    vis_value,
    vis_out,
    w_proj,
    text_embed,
    slots,
    lengths,
    attn_gain,
    mlp_gain,
    w_kv,
    w_gate,
    w_up,
    w_down,
):
    segment, corners = image_tables(grids[0])
    normed = layer_norm(patches, vis_gain)
    query_rows = jnp.dot(normed, vis_query, preferred_element_type=jnp.float32).astype(jnp.bfloat16)
    key_rows = jnp.dot(normed, vis_key, preferred_element_type=jnp.float32).astype(jnp.bfloat16)
    value_rows = jnp.dot(normed, vis_value, preferred_element_type=jnp.float32).astype(jnp.bfloat16)
    slot_count = patches.shape[0]
    head_count = query_rows.shape[1] // VHD
    head_query = query_rows.reshape(slot_count, head_count, VHD)
    head_key = key_rows.reshape(slot_count, head_count, VHD)
    head_value = value_rows.reshape(slot_count, head_count, VHD)
    scores = jnp.einsum(
        "qhd,khd->hqk", head_query, head_key, preferred_element_type=jnp.float32
    ) * VHD ** (-0.5)
    allowed = segment[:, None] == segment[None, :]
    scores = jnp.where(allowed[None, :, :], scores, -1e30)
    row_max = jnp.max(scores, axis=-1, keepdims=True)
    expos = jnp.exp(scores - row_max)
    attn_probs = (expos / jnp.sum(expos, axis=-1, keepdims=True)).astype(jnp.bfloat16)
    context = jnp.einsum("hqk,khd->qhd", attn_probs, head_value, preferred_element_type=jnp.float32)
    context = context.reshape(slot_count, head_count * VHD).astype(jnp.bfloat16)
    partial_out = jnp.dot(context, vis_out, preferred_element_type=jnp.float32)
    attended = lax.psum(partial_out.astype(jnp.bfloat16), "grp").astype(jnp.float32)
    vision = (patches.astype(jnp.float32) + attended).astype(jnp.bfloat16)
    merged = vision[corners.reshape(-1)].reshape(corners.shape[0], 4 * patches.shape[1])
    tok_dev = text_embed.shape[0]
    tp_count = lax.axis_size("tp")
    half_tok = tok_dev * tp_count
    group_index = lax.axis_index("grp")
    tp_index = lax.axis_index("tp")
    col_count = w_proj.shape[1]
    image_cols = jnp.dot(
        lax.all_gather(merged, "tp", axis=0, tiled=True), w_proj, preferred_element_type=jnp.float32
    ).astype(jnp.bfloat16)
    local_rows = positions - group_index * half_tok
    inside = (local_rows >= 0) & (local_rows < half_tok)
    local_rows = jnp.where(inside, local_rows, half_tok)
    buffer = (
        jnp.zeros((half_tok, col_count), jnp.bfloat16).at[local_rows].set(image_cols, mode="drop")
    )
    placed = lax.all_to_all(buffer, "tp", split_axis=0, concat_axis=1, tiled=True)
    first_row = (group_index * tp_count + tp_index) * tok_dev
    own_rows = first_row + jnp.arange(tok_dev, dtype=jnp.int32)
    is_image = jnp.any(positions[None, :] == own_rows[:, None], axis=1)
    assembled = jnp.where(is_image[:, None], placed, text_embed)
    token_batch = lax.all_gather(assembled, "tp", axis=0, tiled=True)
    mlp_normed = rms_norm(token_batch, mlp_gain)
    gate_val = jnp.dot(mlp_normed, w_gate, preferred_element_type=jnp.float32)
    up_val = jnp.dot(mlp_normed, w_up, preferred_element_type=jnp.float32)
    hidden = (jax.nn.silu(gate_val) * up_val).astype(jnp.bfloat16)
    every_term = jnp.dot(hidden, w_down, preferred_element_type=jnp.float32)
    every_sum = lax.psum(every_term, "tp")
    mixed = lax.dynamic_slice_in_dim(every_sum, tp_index * tok_dev, tok_dev, 0)
    layer_out = (assembled.astype(jnp.float32) + mixed).astype(jnp.bfloat16)
    slot_ids = slots[0]
    slot_rows = token_batch[slot_ids]
    attn_normed = rms_norm(slot_rows, attn_gain)
    kv_cols = jnp.dot(attn_normed, w_kv, preferred_element_type=jnp.float32)
    token_pos = slot_positions(slot_ids, lengths[0])
    kv_out = rotate_keys(kv_cols, token_pos, tp_index * w_kv.shape[1]).astype(jnp.bfloat16)
    return (layer_out, kv_out[None])


def solution(mesh):
    return jax.shard_map(
        local,
        mesh=mesh,
        in_specs=(
            P("tp", None),
            P("tp", None, None),
            P(),
            P(),
            P(None, "grp"),
            P(None, "grp"),
            P(None, "grp"),
            P("grp", None),
            P(None, "tp"),
            P(("grp", "tp"), None),
            P("grp", None),
            P("grp", None),
            P(),
            P(),
            P(None, "tp"),
            P(None, "tp"),
            P(None, "tp"),
            P("tp", None),
        ),
        out_specs=(P(("grp", "tp"), None), P("grp", None, "tp")),
        check_vma=False,
    )
```

profile of v0, /device:TPU:0, one launch (start us, length us, event | category | flops | bytes accessed | tf_op | source)
XLA Modules:
  0.0 1008.2 jit_solution(15142676936785822267)
XLA Ops:
  7.3 1.2 convert_reduce_fusion
  8.5 1.2 fusion.35
  10.8 2.4 convolution_convert_fusion.4
  13.5 2.4 convolution_convert_fusion.3
  16.5 2.4 convolution_convert_fusion.5
  19.6 1.2 convolution_convert_fusion
  22.9 29.8 %all-reduce.3.cloned.1.call-done = bf16[80,1408]{1,0:T(8,128)(2,1)} async-done(((bf16[80,1408]{1,0:T(8,128)(2,1)}), bf16[80,1408]{1,0:T(8,128)(2,1)}) %all-reduce.3.cloned.1.call-update) | async-done | bytes 225296 | tf_op jit(solution)/shard_map/psum | solution.py:120
  52.7 1.0 fusion.38
  55.4 109.3 %all-gather.6.cloned.1.call-done = bf16[64,20,5632]{2,1,0:T(8,128)(2,1)} async-done(((bf16[1,20,5632]{2,1,0:T(8,128)(2,1)}), bf16[64,20,5632]{2,1,0:T(8,128)(2,1)}) %all-gather.6.cloned.1.call-update) | async-done | bytes 14417936 | tf_op jit(solution)/shard_map/all_gather | solution.py:130
  164.7 17.6 %reshape.654 = bf16[1280,5632]{1,0:T(8,128)(2,1)} reshape(bf16[64,20,5632]{2,1,0:T(8,128)(2,1)} %all-gather.6.cloned.1.call-done) | data formatting | bytes 28835840
  182.2 9.6 convolution_convert_fusion.1
  192.0 6.3 scatter_custom_fusion
  199.2 6.1 all-to-all-start
  205.5 9.7 all-to-all-done
  216.8 77.8 %all-gather.4.cloned.1.call-done = bf16[1024,4096]{1,0:T(8,128)(2,1)} async-done(((bf16[16,4096]{1,0:T(8,128)(2,1)}), bf16[1024,4096]{1,0:T(8,128)(2,1)}) %all-gather.4.cloned.1.call-update) | async-done | bytes 8388624 | tf_op jit(solution)/shard_map/all_gather | solution.py:143
  294.6 5.2 fusion.1
  300.4 4.7 fusion.13
  305.1 11.7 %fusion.22 = f32[1024,4096]{1,0:T(8,128)} fusion(bf16[172,4096]{1,0:T(8,128)(2,1)} %param.35, bf16[4096,172]{0,1:T(8,128)(2,1)S(1)} %copy-done.4, bf16[1024,4096]{1,0:T(8,128)(2,1)} %all-gather.4.cloned.1.call-done, f32[4096]{0:T(1024)S(1)} %copy-done.8, f32[1024]{0:T(1024)S(1)} %add_rsqrt_fusion, f32[1024,172]{0,1:T(8,128)S(1)} %fusion.13), kind=kOutput, calls=%fused_computation.23 | convolution fusion | flops 2903515136 | bytes 28708864 | tf_op jit(solution)/shard_map/dot_general | solution.py:148
  317.9 13.0 %gather_fusion.1 = bf16[512,4096]{1,0:T(8,128)(2,1)} fusion(bf16[1024,4096]{1,0:T(8,128)(2,1)} %all-gather.4.cloned.1.call-done, s32[1024]{0:T(1024)S(1)} %pad_clamp_fusion), kind=kCustom, calls=%fused_computation.1 | custom fusion | bytes 8390656 | tf_op jit(solution)/shard_map/gather | solution.py:153
  330.9 3.3 fusion.4
  334.2 4.2 fusion.7
  338.5 4.5 subtract_convert_fusion
  344.2 655.8 %all-reduce.5.cloned.1.call-done = f32[1024,4096]{1,0:T(8,128)} async-done(((f32[1024,4096]{1,0:T(8,128)}), f32[1024,4096]{1,0:T(8,128)}) %all-reduce.5.cloned.1.call-update) | async-done | bytes 16777232 | tf_op jit(solution)/shard_map/psum | solution.py:149
  1000.0 1.6 add_convert_fusion
  (89 shorter events, 11.9 us)
Async XLA Ops:
  7.2 12.4 %copy-start = (bf16[704,1408]{1,0:T(8,128)(2,1)S(1)}, bf16[704,1408]{1,0:T(8,128)(2,1)}, u32[]{:S(2)}) copy-start(bf16[704,1408]{1,0:T(8,128)(2,1)} %param.25) | copy-start | bytes 5947396
  7.2 45.5 %copy-start.3 = (bf16[80,1408]{1,0:T(8,128)(2,1)S(1)}, bf16[80,1408]{1,0:T(8,128)(2,1)}, u32[]{:S(2)}) copy-start(bf16[80,1408]{1,0:T(8,128)(2,1)} %param.18) | copy-start | bytes 675844
  7.2 14.4 %copy-start.11 = (s32[1,3,2]{1,2,0:T(2,128)S(1)}, s32[1,3,2]{1,2,0:T(2,128)}, u32[]{:S(2)}) copy-start(s32[1,3,2]{1,2,0:T(2,128)} %param.19) | copy-start | bytes 76
  7.2 45.5 %all-reduce.3.cloned.1.call-start = ((), (), s32[]{:S(2)}) async-start(), calls=%async_computation.1 | async-start | bytes 450560 | tf_op jit(solution)/shard_map/psum | solution.py:120
  10.8 44.6 %copy-start.9 = (s32[1280]{0:T(1024)S(1)}, s32[1280]{0:T(1024)}, u32[]{:S(2)}) copy-start(s32[1280]{0:T(1024)} %param.20) | copy-start | bytes 15364
  20.8 143.9 %all-gather.6.cloned.1.call-start = ((), (), s32[]{:S(2)}) async-start(), calls=%async_computation.4 | async-start | bytes 17571840 | tf_op jit(solution)/shard_map/all_gather | solution.py:130
  55.4 126.8 %copy-start.6 = (bf16[5632,64]{0,1:T(8,128)(2,1)S(1)}, bf16[5632,64]{0,1:T(8,128)(2,1)}, u32[]{:S(2)}) copy-start(bf16[5632,64]{0,1:T(8,128)(2,1)} %param.26) | copy-start | bytes 2162692
  182.2 33.6 %copy-start.7 = (bf16[16,4096]{1,0:T(8,128)(2,1)S(1)}, bf16[16,4096]{1,0:T(8,128)(2,1)}, u32[]{:S(2)}) copy-start(bf16[16,4096]{1,0:T(8,128)(2,1)} %param.27) | copy-start | bytes 393220
  191.8 108.1 %copy-start.8 = (f32[4096]{0:T(1024)S(1)}, f32[4096]{0:T(1024)}, u32[]{:S(2)}) copy-start(f32[4096]{0:T(1024)} %param.31) | copy-start | bytes 49156
  199.2 16.1 %all-to-all-start = ((bf16[64,2,512]{2,1,0:T(2,128)(2,1)}), bf16[64,2,512]{2,1,0:T(2,128)(2,1)S(1)}, u32[]{:S(2)}, u32[]{:S(2)}) async-start(bf16[64,2,512]{2,1,0:T(2,128)(2,1)} %reshape.658), calls=%async_computation | async-start | bytes 262144 | tf_op jit(solution)/shard_map/all_to_all | solution.py:138
  205.3 89.3 %all-gather.4.cloned.1.call-start = ((), (), s32[]{:S(2)}) async-start(), calls=%async_computation.2 | async-start | bytes 8519680 | tf_op jit(solution)/shard_map/all_gather | solution.py:143
  216.6 783.4 %all-reduce.5.cloned.1.call-start = ((), (), s32[]{:S(2)}) async-start(), calls=%async_computation.3 | async-start | bytes 33554432 | tf_op jit(solution)/shard_map/psum | solution.py:149
  294.6 5.8 copy-start.2
  300.4 4.7 copy-start.4
  316.9 0.7 copy-start.13
  316.9 0.9 copy-start.10
  317.9 16.3 %copy-start.12 = (f32[4096]{0:T(1024)S(1)}, f32[4096]{0:T(1024)}, u32[]{:S(2)}) copy-start(f32[4096]{0:T(1024)} %param.30) | copy-start | bytes 49156
  330.9 669.1 %copy-start.5 = (bf16[16,4096]{1,0:T(8,128)(2,1)S(1)}, bf16[16,4096]{1,0:T(8,128)(2,1)}, u32[]{:S(2)}) copy-start(bf16[16,4096]{1,0:T(8,128)(2,1)} %broadcast_select_fusion.2) | copy-start | bytes 393220
  330.9 670.7 %copy-start.1 = (bf16[704,1408]{1,0:T(8,128)(2,1)S(1)}, bf16[704,1408]{1,0:T(8,128)(2,1)}, u32[]{:S(2)}) copy-start(bf16[704,1408]{1,0:T(8,128)(2,1)} %param.25) | copy-start | bytes 5947396
Sparse Core Ops, SparseCore 0:
  20.9 31.7 all-reduce.2
  56.0 108.6 all-gather.5
  216.7 77.8 all-gather.3
  317.0 682.9 all-reduce.4
where the time goes:
time: 1010 us
  waiting for transfers between devices  883 us (87%)
  local copies, waits for them, and re-layouts  43.9 us (4%)
  matrix products  39.2 us (4%)
  other arithmetic  22 us (2%)
  between operations  14.2 us (1%)
    psum x1, waiting for transfers between devices, local(): every_sum = lax.psum(every_term, 'tp')  656 us
    all_gather x1, waiting for transfers between devices, local(): lax.all_gather(merged, 'tp', axis=0, tiled=True)  109 us
    all_gather x1, waiting for transfers between devices, local(): token_batch = lax.all_gather(assembled, 'tp', axis=0, tiled=True)  77.8 us
    psum x1, waiting for transfers between devices, local(): lax.psum(partial_out.astype(jnp.bfloat16), 'grp').astype(jnp.float32)  29.8 us
    unnamed x33, local copies, waits for them, and re-layouts  21.5 us
  transfers between devices with their start and end apart: 5, of which 5 were waited for; matrix products, arithmetic and copies ran while one was open for 3% of the time, Pallas kernels for 0%

commit v1 on v0

--- a/solution.py
+++ b/solution.py
@@ -3,6 +3,8 @@
 import jax
 import jax.numpy as jnp
 from jax import lax
+from jax.experimental import pallas as pl
+from jax.experimental.pallas import tpu as pltpu
 from jax.sharding import PartitionSpec as P
 
 VHD = 88
@@ -51,22 +53,13 @@
     return (segment, jnp.where(valid[:, None], corners, 0))
 
 
-def rotate_keys(values_f, token_pos, first_col):
-    col_count = values_f.shape[1]
-    col_ids = first_col + jnp.arange(0, col_count, 2, dtype=jnp.int32)
-    pair_ids = col_ids % HD // 2
-    is_key = col_ids // HD % 2 == 0
+def rotation_tables(token_pos):
+    pair_ids = jnp.arange(HD, dtype=jnp.int32) // 2
     freq = jnp.exp(pair_ids.astype(jnp.float32) * (-2.0 * math.log(10000.0) / HD))
     angle = token_pos.astype(jnp.float32)[:, None] * freq[None, :]
-    cosine = jnp.where(is_key[None, :], jnp.cos(angle), 1.0)
-    sine = jnp.where(is_key[None, :], jnp.sin(angle), 0.0)
-    paired = values_f.reshape(values_f.shape[0], col_count // 2, 2)
-    even_part = paired[:, :, 0]
-    odd_part = paired[:, :, 1]
-    turned = jnp.stack(
-        [even_part * cosine - odd_part * sine, even_part * sine + odd_part * cosine], axis=2
-    )
-    return turned.reshape(values_f.shape[0], col_count)
+    odd = jnp.arange(HD, dtype=jnp.int32)[None, :] % 2 == 1
+    sine = jnp.sin(angle)
+    return jnp.cos(angle), jnp.where(odd, sine, -sine)
 
 
 def slot_positions(slot_ids, length_row):
@@ -74,6 +67,411 @@
     req_starts = req_ends - length_row
     inside = (slot_ids[:, None] >= req_starts[None, :]) & (slot_ids[:, None] < req_ends[None, :])
     return slot_ids - jnp.sum(jnp.where(inside, req_starts[None, :], 0), axis=1)
+
+
+MESH = pl.DeviceIdType.MESH
+BF = jnp.bfloat16
+F32 = jnp.float32
+D = 4096
+UNITS = 172
+CHIPS = 32
+ROWS = 512
+OWN = 16
+STEP = 1024
+
+
+class Place:
+    def __init__(self):
+        index = lax.axis_index("tp")
+        self.core = lax.rem(index, 2)
+        self.x = lax.rem(lax.div(index, 2), 4)
+        self.z = lax.rem(lax.div(index, 8), 4)
+        self.yh = lax.div(index, 32)
+
+    def chip(self, far, dz, dx):
+        yh = 1 - self.yh if far else self.yh
+        return (yh * 4 + lax.rem(self.z + dz + 4, 4)) * 4 + lax.rem(self.x + dx + 4, 4)
+
+    def device(self, far, dz, dx, other_core=False):
+        core = 1 - self.core if other_core else self.core
+        return self.chip(far, dz, dx) * 2 + core
+
+    def along(self, order, far, first, second):
+        return self.chip(far, second, first) if order == 0 else self.chip(far, first, second)
+
+    def step(self, order, stage, sign):
+        along_x = (order == 0) == (stage == 0)
+        return self.device(False, 0, sign) if along_x else self.device(False, sign, 0)
+
+
+def greet(place):
+    barrier = pltpu.get_barrier_semaphore()
+    peers = [
+        place.device(False, 0, 1),
+        place.device(False, 0, -1),
+        place.device(False, 1, 0),
+        place.device(False, -1, 0),
+        place.device(True, 0, 0),
+        place.device(False, 0, 0, other_core=True),
+    ]
+    for peer in peers:
+        pl.semaphore_signal(barrier, inc=1, device_id={"tp": peer}, device_id_type=MESH)
+    pl.semaphore_wait(barrier, len(peers))
+
+
+class Mail:
+    def __init__(self, send_sems, recv_sems):
+        self.send_sems = send_sems
+        self.recv_sems = recv_sems
+        self.sent = []
+
+    def send(self, src, dst, peer):
+        number = len(self.sent)
+        copy = pltpu.make_async_remote_copy(
+            src_ref=src,
+            dst_ref=dst,
+            send_sem=self.send_sems.at[number],
+            recv_sem=self.recv_sems.at[number],
+            device_id={"tp": peer},
+            device_id_type=MESH,
+        )
+        copy.start()
+        self.sent.append(copy)
+        return copy
+
+    def finish(self):
+        for copy in self.sent:
+            copy.wait_send()
+
+
+class Gather:
+    def __init__(self, place, mail, view, whole):
+        self.place, self.mail, self.view, self.whole = place, mail, view, whole
+
+    def pair_start(self):
+        ref = self.whole(self.place.chip(False, 0, 0))
+        self.pair = self.mail.send(ref, ref, self.place.device(True, 0, 0))
+
+    def pair_wait(self):
+        self.pair.wait_recv()
+
+    def pass_on(self, order, far, first, second, quarter, stage, sign):
+        ref = self.view(self.place.along(order, far, first, second), order, quarter)
+        return self.mail.send(ref, ref, self.place.step(order, stage, sign))
+
+    def open(self, far):
+        state = {}
+        for order in (0, 1):
+            for sign in (1, -1):
+                state[order, 0, sign] = self.pass_on(order, far, 0, 0, None, 0, sign)
+        for order in (0, 1):
+            self.spread(state, order, far, 0)
+        return state
+
+    def spread(self, state, order, far, first):
+        for sign in (1, -1):
+            state[order, 1, first, sign] = self.pass_on(order, far, first, 0, None, 1, sign)
+
+    def near(self, state, far):
+        for order in (0, 1):
+            for sign, quarter in ((1, 0), (-1, 1)):
+                state[order, 0, sign].wait_recv()
+                state[order, 2, sign] = self.pass_on(order, far, -sign, 0, quarter, 0, sign)
+        for order in (0, 1):
+            self.spread(state, order, far, 1)
+            self.spread(state, order, far, -1)
+
+    def opposite(self, state, far):
+        for order in (0, 1):
+            for sign in (1, -1):
+                state[order, 2, sign].wait_recv()
+        for order in (0, 1):
+            self.spread(state, order, far, 2)
+
+    def relay(self, state, far, first):
+        for order in (0, 1):
+            for sign, quarter in ((1, 0), (-1, 1)):
+                state[order, 1, first, sign].wait_recv()
+                state[order, 3, first, sign] = self.pass_on(
+                    order, far, first, -sign, quarter, 1, sign
+                )
+
+    def close(self, state):
+        for order in (0, 1):
+            for first in (0, 1, -1, 2):
+                for sign in (1, -1):
+                    state[order, 3, first, sign].wait_recv()
+
+    def run(self):
+        self.pair_start()
+        here = self.open(False)
+        self.near(here, False)
+        self.opposite(here, False)
+        self.relay(here, False, 0)
+        self.pair_wait()
+        there = self.open(True)
+        self.relay(here, False, 1)
+        self.relay(here, False, -1)
+        self.near(there, True)
+        self.relay(here, False, 2)
+        self.opposite(there, True)
+        self.close(here)
+        for first in (0, 1, -1, 2):
+            self.relay(there, True, first)
+        self.close(there)
+
+
+class Scatter:
+    def __init__(self, place, mail, sums, halves, wholes, pair):
+        self.place, self.mail = place, mail
+        self.sums, self.halves, self.wholes, self.pair = sums, halves, wholes, pair
+
+    def view(self, chip, order, quarter):
+        width = D // 4
+        if quarter is None:
+            return self.sums.at[chip, :, pl.ds(order * 2 * width, 2 * width)]
+        return self.sums.at[chip, :, pl.ds((2 * order + quarter) * width, width)]
+
+    def lines(self, stage):
+        return (0, 1, 2, 3) if stage == 0 else (4,)
+
+    def chip(self, order, far, stage, line, second):
+        if stage == 0:
+            return self.place.along(order, far, line, second)
+        return self.place.along(order, far, second, 0)
+
+    def open(self, far, order, stage):
+        state = {}
+        for line in self.lines(stage):
+            chip = self.chip(order, far, stage, line, 2)
+            for side, sign in ((0, -1), (1, 1)):
+                slot = self.halves.at[int(far), order, line, side]
+                state[line, 0, side] = self.mail.send(
+                    self.view(chip, order, side), slot, self.place.step(order, 1 - stage, sign)
+                )
+        return state
+
+    def add(self, chip, order, quarter, terms):
+        ref = self.view(chip, order, quarter)
+        total = ref[...].astype(F32)
+        for term in terms:
+            total = total + term[...].astype(F32)
+        ref[...] = total.astype(BF)
+
+    def middle(self, state, far, order, stage):
+        for line in self.lines(stage):
+            for side, sign in ((0, -1), (1, 1)):
+                state[line, 0, side].wait_recv()
+                chip = self.chip(order, far, stage, line, sign)
+                self.add(chip, order, side, [self.halves.at[int(far), order, line, side]])
+                slot = self.wholes.at[int(far), order, line, side]
+                state[line, 1, side] = self.mail.send(
+                    self.view(chip, order, None), slot, self.place.step(order, 1 - stage, sign)
+                )
+
+    def close(self, state, far, order, stage):
+        for line in self.lines(stage):
+            for side in (0, 1):
+                state[line, 1, side].wait_recv()
+            chip = self.chip(order, far, stage, line, 0)
+            self.add(
+                chip, order, None, [self.wholes.at[int(far), order, line, side] for side in (0, 1)]
+            )
+
+
+def feed_forward(
+    block_ref,
+    mlp_gain,
+    attn_gain,
+    gate_ref,
+    up_ref,
+    down_ref,
+    kv_w_ref,
+    cos_ref,
+    sin_ref,
+    slot_ref,
+    out_ref,
+    kv_ref,
+    tokens,
+    first_w,
+    down_w,
+    kv_w,
+    first_acc,
+    kv_acc,
+    squares,
+    hidden,
+    sums,
+    halves,
+    wholes,
+    pair_slot,
+    kv_all,
+    kv_part,
+    send_sems,
+    recv_sems,
+    local_sems,
+):
+    place = Place()
+    mail = Mail(send_sems, recv_sems)
+    core = place.core
+    mine = place.chip(False, 0, 0)
+    other = place.device(False, 0, 0, other_core=True)
+
+    block_copy = pltpu.make_async_copy(block_ref, tokens.at[mine], local_sems.at[0])
+    block_copy.start()
+    kv_cols = pl.ds(pl.multiple_of(core * HD, HD), HD)
+    targets = [
+        (gate_ref, first_w.at[core]),
+        (up_ref, first_w.at[2 + core]),
+        (down_ref, down_w.at[core]),
+        (kv_w_ref, kv_w.at[:, kv_cols]),
+    ]
+    local_copies = []
+    for number, (source, target) in enumerate(targets):
+        copy = pltpu.make_async_copy(source, target, local_sems.at[1 + number])
+        copy.start()
+        local_copies.append(copy)
+    block_copy.wait()
+    greet(place)
+
+    def cut(chip, order, quarter):
+        if quarter is None:
+            return tokens.at[chip, pl.ds(order * 256, 256)]
+        return tokens.at[chip, pl.ds(order * 256 + quarter * 128, 128)]
+
+    gather = Gather(place, mail, cut, lambda chip: tokens.at[chip])
+    weight_mail = [mail.send(source, target, other) for source, target in targets]
+    gather.run()
+    for copy in local_copies:
+        copy.wait()
+    for copy in weight_mail:
+        copy.wait_recv()
+
+    first_acc[...] = jnp.zeros_like(first_acc)
+    kv_acc[...] = jnp.zeros_like(kv_acc)
+    squares[...] = jnp.zeros_like(squares)
+    contract = (((1,), (1,)), ((), ()))
+
+    def accumulate(step, _):
+        cols = pl.ds(pl.multiple_of(step * STEP, STEP), STEP)
+        rows = jnp.concatenate([tokens[step * 8 + j] for j in range(8)], axis=1).astype(F32)
+        part = rows * rows
+        for j in range(8):
+            squares[...] += part[:, j * 128 : (j + 1) * 128]
+        scaled = (rows * mlp_gain[pl.ds(step, 1), :]).astype(BF)
+        for part in range(4):
+            first_acc[part] += lax.dot_general(
+                scaled, first_w[part, :, cols], contract, preferred_element_type=F32
+            )
+        scaled = (rows * attn_gain[pl.ds(step, 1), :]).astype(BF)
+        kv_acc[...] += jnp.dot(scaled, kv_w[cols, :], preferred_element_type=F32)
+        return 0
+
+    lax.fori_loop(0, D // STEP, accumulate, 0)
+    mean_square = jnp.sum(squares[...], axis=1, keepdims=True) * (1.0 / D)
+    inverse = lax.rsqrt(mean_square + 1e-05)
+    for part in (0, 1):
+        gate_val = first_acc[part] * inverse
+        up_val = first_acc[2 + part] * inverse
+        hidden[part] = (gate_val / (1.0 + jnp.exp(-gate_val)) * up_val).astype(BF)
+
+    def project(step, _):
+        cols = pl.ds(pl.multiple_of(step * 512, 512), 512)
+        part = jnp.dot(hidden[0], down_w[0, :, cols], preferred_element_type=F32)
+        part = part + jnp.dot(hidden[1], down_w[1, :, cols], preferred_element_type=F32)
+        sums[:, :, cols] = part.astype(BF).reshape(CHIPS, OWN, 512)
+        return 0
+
+    lax.fori_loop(0, D // 512, project, 0)
+
+    scatter = Scatter(place, mail, sums, halves, wholes, pair_slot)
+    keys = (True, 0), (True, 1), (False, 0), (False, 1)
+    outer = {key: scatter.open(key[0], key[1], 0) for key in keys}
+
+    turn = kv_acc[...] * inverse
+    key_part = turn[:, :HD]
+    lane = lax.broadcasted_iota(jnp.int32, key_part.shape, 1)
+    partner = jnp.where(
+        lax.rem(lane, 2) == 0,
+        pltpu.roll(key_part, HD - 1, axis=1),
+        pltpu.roll(key_part, 1, axis=1),
+    )
+    key_part = (key_part * cos_ref[...] + partner * sin_ref[...]).astype(BF)
+    value_part = turn[:, HD:].astype(BF)
+    my_rows = pl.ds(pl.multiple_of(core * ROWS, ROWS), ROWS)
+    first_core = core == 0
+    kv_all[my_rows, :] = jnp.where(first_core, key_part, value_part)
+    kv_part[...] = jnp.where(first_core, value_part, key_part)
+    kv_mail = mail.send(kv_part, kv_all.at[my_rows], other)
+
+    for key in keys:
+        scatter.middle(outer[key], key[0], key[1], 0)
+    inner = {}
+    for key in keys:
+        scatter.close(outer[key], key[0], key[1], 0)
+        inner[key] = scatter.open(key[0], key[1], 1)
+    kv_mail.wait_recv()
+    pick = lax.broadcasted_iota(jnp.int32, (ROWS, 2 * ROWS), 1) == slot_ref[...]
+    kv_ref[...] = jnp.dot(
+        pick.astype(F32).astype(BF), kv_all[...], preferred_element_type=F32
+    ).astype(BF)
+    for key in keys:
+        scatter.middle(inner[key], key[0], key[1], 1)
+    for key in keys[:2]:
+        scatter.close(inner[key], key[0], key[1], 1)
+    pair_mail = mail.send(
+        sums.at[place.chip(True, 0, 0)], pair_slot, place.device(True, 0, 0)
+    )
+    for key in keys[2:]:
+        scatter.close(inner[key], key[0], key[1], 1)
+    own_rows = pl.ds(pl.multiple_of(mine * OWN, OWN), OWN)
+    pair_mail.wait_recv()
+    for chip in range(CHIPS):
+        cols = slice(chip * 128, (chip + 1) * 128)
+        mixed = sums[mine, :, cols].astype(F32) + pair_slot[:, cols].astype(F32)
+        out_ref[:, cols] = (tokens[chip, own_rows, :].astype(F32) + mixed).astype(BF)
+    mail.finish()
+
+
+def feed_forward_call(block, mlp_gain, attn_gain, gate_t, up_t, down, kv_w, cosine, sine, slot_row):
+    anywhere = pl.BlockSpec(memory_space=pl.ANY)
+    local = pl.BlockSpec(memory_space=pltpu.VMEM)
+    return pl.pallas_call(
+        feed_forward,
+        out_shape=(
+            jax.ShapeDtypeStruct((OWN, D), BF),
+            jax.ShapeDtypeStruct((ROWS, HD), BF),
+        ),
+        in_specs=[anywhere, local, local, anywhere, anywhere, anywhere, anywhere, local, local, local],
+        out_specs=(local, local),
+        scratch_shapes=[
+            pltpu.VMEM((CHIPS, ROWS, 128), BF),
+            pltpu.VMEM((4, UNITS, D), BF),
+            pltpu.VMEM((2, UNITS, D), BF),
+            pltpu.VMEM((D, 2 * HD), BF),
+            pltpu.VMEM((4, ROWS, UNITS), F32),
+            pltpu.VMEM((ROWS, 2 * HD), F32),
+            pltpu.VMEM((ROWS, 128), F32),
+            pltpu.VMEM((2, ROWS, UNITS), BF),
+            pltpu.VMEM((CHIPS, OWN, D), BF),
+            pltpu.VMEM((2, 2, 5, 2, OWN, D // 4), BF),
+            pltpu.VMEM((2, 2, 5, 2, OWN, D // 2), BF),
+            pltpu.VMEM((OWN, D), BF),
+            pltpu.VMEM((2 * ROWS, HD), BF),
+            pltpu.VMEM((ROWS, HD), BF),
+            pltpu.SemaphoreType.DMA((176,)),
+            pltpu.SemaphoreType.DMA((176,)),
+            pltpu.SemaphoreType.DMA((5,)),
+        ],
+        compiler_params=pltpu.CompilerParams(
+            collective_id=1, has_side_effects=True, vmem_limit_bytes=63 * 1024 * 1024
+        ),
+        name="feed_forward",
+    )(block, mlp_gain, attn_gain, gate_t, up_t, down, kv_w, cosine, sine, slot_row)
+
+
+def own_core_tokens(core):
+    local_row = jnp.arange(ROWS, dtype=jnp.int32)
+    return (local_row // OWN * 2 + core) * OWN + local_row % OWN
 
 
 def local(
@@ -125,6 +523,7 @@
     half_tok = tok_dev * tp_count
     group_index = lax.axis_index("grp")
     tp_index = lax.axis_index("tp")
+    core = tp_index % 2
     col_count = w_proj.shape[1]
     image_cols = jnp.dot(
         lax.all_gather(merged, "tp", axis=0, tiled=True), w_proj, preferred_element_type=jnp.float32
@@ -135,26 +534,34 @@
     buffer = (
         jnp.zeros((half_tok, col_count), jnp.bfloat16).at[local_rows].set(image_cols, mode="drop")
     )
-    placed = lax.all_to_all(buffer, "tp", split_axis=0, concat_axis=1, tiled=True)
-    first_row = (group_index * tp_count + tp_index) * tok_dev
-    own_rows = first_row + jnp.arange(tok_dev, dtype=jnp.int32)
-    is_image = jnp.any(positions[None, :] == own_rows[:, None], axis=1)
-    assembled = jnp.where(is_image[:, None], placed, text_embed)
-    token_batch = lax.all_gather(assembled, "tp", axis=0, tiled=True)
-    mlp_normed = rms_norm(token_batch, mlp_gain)
-    gate_val = jnp.dot(mlp_normed, w_gate, preferred_element_type=jnp.float32)
-    up_val = jnp.dot(mlp_normed, w_up, preferred_element_type=jnp.float32)
-    hidden = (jax.nn.silu(gate_val) * up_val).astype(jnp.bfloat16)
-    every_term = jnp.dot(hidden, w_down, preferred_element_type=jnp.float32)
-    every_sum = lax.psum(every_term, "tp")
-    mixed = lax.dynamic_slice_in_dim(every_sum, tp_index * tok_dev, tok_dev, 0)
-    layer_out = (assembled.astype(jnp.float32) + mixed).astype(jnp.bfloat16)
+    is_image = jnp.zeros((half_tok,), jnp.int32).at[local_rows].set(1, mode="drop")
+    text_cols = lax.all_to_all(text_embed, "tp", split_axis=1, concat_axis=0, tiled=True)
+    columns = jnp.where(is_image[:, None] > 0, buffer, text_cols)
+    by_core = columns.reshape(tp_count // 2, 2, tok_dev, col_count)
+    mine = lax.dynamic_index_in_dim(by_core, core, 1, keepdims=False).reshape(ROWS, col_count)
+    theirs = lax.dynamic_index_in_dim(by_core, 1 - core, 1, keepdims=False).reshape(ROWS, col_count)
+    swap = [(index, index ^ 1) for index in range(tp_count)]
+    came = lax.ppermute(theirs, "tp", swap)
+    block = jnp.where(
+        core == 0, jnp.concatenate([mine, came], 1), jnp.concatenate([came, mine], 1)
+    )
+
+    token_pos = slot_positions(own_core_tokens(core), lengths[0])
+    cosine, sine = rotation_tables(token_pos)
     slot_ids = slots[0]
-    slot_rows = token_batch[slot_ids]
-    attn_normed = rms_norm(slot_rows, attn_gain)
-    kv_cols = jnp.dot(attn_normed, w_kv, preferred_element_type=jnp.float32)
-    token_pos = slot_positions(slot_ids, lengths[0])
-    kv_out = rotate_keys(kv_cols, token_pos, tp_index * w_kv.shape[1]).astype(jnp.bfloat16)
+    slot_row = slot_ids // OWN % 2 * ROWS + slot_ids // (2 * OWN) * OWN + slot_ids % OWN
+    layer_out, kv_out = feed_forward_call(
+        block,
+        mlp_gain.reshape(D // STEP, STEP),
+        attn_gain.reshape(D // STEP, STEP),
+        w_gate.T,
+        w_up.T,
+        w_down,
+        w_kv,
+        cosine,
+        sine,
+        slot_row[:, None],
+    )
     return (layer_out, kv_out[None])
 
 

time: 1010 us -> 287 us (0.28)
  waiting for transfers between devices: 883 us -> 120 us
  Pallas kernels: 0 us -> 73.3 us
  matrix products: 39.2 us -> 17.9 us
  other arithmetic: 22 us -> 10.1 us
    psum x1 -> x0, waiting for transfers between devices: 656 us -> none  [local(): every_sum = lax.psum(every_term, 'tp')]
    all_gather x1 -> x0, waiting for transfers between devices: 77.8 us -> none  [local(): token_batch = lax.all_gather(assembled, 'tp', axis=0, tiled=True)]
    pallas_call x0 -> x1, Pallas kernels: none -> 73.3 us  [feed_forward_call(): pl.pallas_call(feed_forward, out_shape=(jax.ShapeDtypeStruct((OWN, D), BF...]
    all_gather x1, waiting for transfers between devices: 109 us -> 87.5 us  [local(): lax.all_gather(merged, 'tp', axis=0, tiled=True)]
    dot_general x3 -> x0, matrix products: 20.6 us -> none  [the longest x1 11.7 us: local(): every_term = jnp.dot(hidden, w_down, preferred_element_type=jnp.float32)]
    gather x1 -> x0, local copies, waits for them, and re-layouts: 13 us -> none  [local(): slot_rows = token_batch[slot_ids]]
    unnamed x33 -> x32, local copies, waits for them, and re-layouts: 21.5 us -> 23.4 us
  transfers between devices with their start and end apart: 5 -> 4, of which waited for: 5 -> 3; matrix products, arithmetic and copies ran while one was open for 3% -> 5% of each run, Pallas kernels for 0% -> 0%
where the time goes in v1:
time: 287 us; the launch traced here: 286 us
  waiting for transfers between devices  120 us (42%)
  Pallas kernels  73.3 us (26%)
  local copies, waits for them, and re-layouts  39.3 us (14%)
  matrix products  17.9 us (6%)
  between operations  14.5 us (5%)
  starting transfers between devices  10.6 us (4%)
  other arithmetic  10.1 us (4%)
    all_gather x1, waiting for transfers between devices, local(): lax.all_gather(merged, 'tp', axis=0, tiled=True)  87.5 us
    pallas_call x1, Pallas kernels, feed_forward_call(): pl.pallas_call(feed_forward, out_shape=(jax.ShapeDtypeStruct((OWN, D), BF...  73.3 us
    psum x1, waiting for transfers between devices, local(): lax.psum(partial_out.astype(jnp.bfloat16), 'grp').astype(jnp.float32)  29.9 us
    unnamed x32, local copies, waits for them, and re-layouts  23.4 us
    all_to_all x1, starting transfers between devices, local(): lax.all_to_all(text_embed, 'tp', split_axis=1, concat_axis=0, tiled=True)  10 us
    dot_general x1, matrix products, local(): jnp.dot(lax.all_gather(merged, 'tp', axis=0, tiled=True), w_proj, preferr...  9.53 us
    scatter x1, local copies, waits for them, and re-layouts, local(): jnp.zeros((half_tok, col_count), jnp.bfloat16).at[local_rows]  6.29 us
  transfers between devices with their start and end apart: 4, of which 3 were waited for; matrix products, arithmetic and copies ran while one was open for 5% of the time, Pallas kernels for 0%

profile of v1, /device:TPU:0, one launch (start us, length us, event | category | flops | bytes accessed | tf_op | source)
XLA Modules:
  0.0 285.7 jit_solution(9536658228708619704)
XLA Ops:
  7.3 0.9 and_select_fusion.6
  8.1 1.1 convert_reduce_fusion
  9.2 1.2 fusion.7
  10.4 2.4 convolution_convert_fusion.4
  15.5 2.4 convolution_convert_fusion.5
  18.1 1.3 fusion.4
  19.7 1.2 convolution_convert_fusion
  23.0 29.9 %all-reduce.2.cloned.1.call-done = bf16[80,1408]{1,0:T(8,128)(2,1)} async-done(((bf16[80,1408]{1,0:T(8,128)(2,1)}), bf16[80,1408]{1,0:T(8,128)(2,1)}) %all-reduce.2.cloned.1.call-update) | async-done | bytes 225296 | tf_op jit(solution)/shard_map/psum | solution.py:518
  52.9 1.0 fusion.10
  54.7 0.9 reshape.624
  56.0 0.8 reshape.631
  56.9 10.0 %all-to-all-start = ((bf16[64,2,512]{2,1,0:T(2,128)(2,1)}), bf16[64,2,512]{2,1,0:T(2,128)(2,1)S(1)}, u32[]{:S(2)}, u32[]{:S(2)}) async-start(bf16[64,2,512]{2,1,0:T(2,128)(2,1)} %reshape.631), calls=%async_computation | async-start | bytes 262144 | tf_op jit(solution)/shard_map/all_to_all | solution.py:538
  67.3 5.2 %scatter_custom_fusion = s32[1024]{0:T(1024)S(1)} fusion(s32[1280]{0:T(1024)S(1)} %compare_select_fusion, s32[1280]{0:T(1024)S(1)} %broadcast.839, s32[]{:T(128)} %constant.164.clone.1), kind=kCustom, calls=%fused_computation.87 | custom fusion | bytes 4100 | tf_op jit(solution)/shard_map/scatter | solution.py:537
  72.7 1.8 negate_select_fusion.7
  74.5 2.6 all-to-all-done
  77.4 87.5 %all-gather.3.cloned.1.call-done = bf16[64,20,5632]{2,1,0:T(8,128)(2,1)} async-done(((bf16[1,20,5632]{2,1,0:T(8,128)(2,1)}), bf16[64,20,5632]{2,1,0:T(8,128)(2,1)}) %all-gather.3.cloned.1.call-update) | async-done | bytes 14417936 | tf_op jit(solution)/shard_map/all_gather | solution.py:529
  164.9 17.6 %reshape.625 = bf16[1280,5632]{1,0:T(8,128)(2,1)} reshape(bf16[64,20,5632]{2,1,0:T(8,128)(2,1)} %all-gather.3.cloned.1.call-done) | data formatting | bytes 28835840
  182.4 9.5 %convolution_convert_fusion.1 = bf16[1280,64]{0,1:T(8,128)(2,1)S(1)} fusion(bf16[1280,5632]{1,0:T(8,128)(2,1)} %reshape.625, bf16[5632,64]{0,1:T(8,128)(2,1)S(1)} %copy-done), kind=kOutput, calls=%fused_computation.5 | convolution fusion | flops 922828800 | bytes 15302656 | tf_op jit(solution)/shard_map/dot_general | solution.py:528
  192.2 6.3 %scatter_custom_fusion.1 = bf16[1024,64]{1,0:T(8,128)(2,1)S(1)} fusion(s32[1280]{0:T(1024)S(1)} %compare_select_fusion, bf16[1280,64]{1,0:T(8,128)(2,1)S(1)} %copy.55, bf16[]{:T(256)} %constant.170.clone.1), kind=kCustom, calls=%fused_computation.56 | custom fusion | bytes 131074 | tf_op jit(solution)/shard_map/scatter | solution.py:535
  199.3 1.1 fusion.14.slot_ref
  201.7 0.8 maximum_select_fusion.block_ref
  202.5 73.3 %feed_forward.1 = (bf16[16,4096]{1,0:T(8,128)(2,1)}, bf16[512,128]{1,0:T(8,128)(2,1)}) custom-call(bf16[512,128]{1,0:T(8,128)(2,1)} %maximum_select_fusion.block_ref, f32[4,1024]{1,0:T(4,128)} %reshape.594.mlp_gain, f32[4,1024]{1,0:T(4,128)} %reshape.595.attn_gain, bf16[172,4096]{1,0:T(8,128)(2,1)} %bitcast.77, bf16[172,4096]{1,0:T(8,128)(2,1)} %bitcast.78, ...), custom_call_target="tpu_custom_call" | custom-call | tf_op jit(solution)/shard_map/feed_forward/pallas_call | solution.py:438
  275.7 1.6 copy.73
  277.3 1.6 copy.74
  (79 shorter events, 9.1 us)
Async XLA Ops:
  7.2 175.3 %copy-start = (bf16[5632,64]{0,1:T(8,128)(2,1)S(1)}, bf16[5632,64]{0,1:T(8,128)(2,1)}, u32[]{:S(2)}) copy-start(bf16[5632,64]{0,1:T(8,128)(2,1)} %param.26) | copy-start | bytes 2162692
  7.2 5.9 %copy-start.1 = (bf16[80,1408]{1,0:T(8,128)(2,1)S(1)}, bf16[80,1408]{1,0:T(8,128)(2,1)}, u32[]{:S(2)}) copy-start(bf16[80,1408]{1,0:T(8,128)(2,1)} %param.18) | copy-start | bytes 675844
  7.2 5.9 %copy-start.5 = (f32[1408]{0:T(1024)S(1)}, f32[1408]{0:T(1024)}, u32[]{:S(2)}) copy-start(f32[1408]{0:T(1024)} %param.21) | copy-start | bytes 16900
  7.2 5.9 %copy-start.2 = (bf16[1408,704]{0,1:T(8,128)(2,1)S(1)}, bf16[1408,704]{0,1:T(8,128)(2,1)}, u32[]{:S(2)}) copy-start(bf16[1408,704]{0,1:T(8,128)(2,1)} %param.23) | copy-start | bytes 5947396
  7.2 45.7 %all-reduce.2.cloned.1.call-start = ((), (), s32[]{:S(2)}) async-start(), calls=%async_computation.1 | async-start | bytes 450560 | tf_op jit(solution)/shard_map/psum | solution.py:518
  14.7 0.7 copy-start.12
  15.5 4.2 %copy-start.3 = (bf16[704,1408]{1,0:T(8,128)(2,1)S(1)}, bf16[704,1408]{1,0:T(8,128)(2,1)}, u32[]{:S(2)}) copy-start(bf16[704,1408]{1,0:T(8,128)(2,1)} %param.25) | copy-start | bytes 5947396
  19.5 1.7 copy-start.9
  20.9 34.7 %copy-start.4 = (bf16[16,4096]{1,0:T(8,128)(2,1)S(1)}, bf16[16,4096]{1,0:T(8,128)(2,1)}, u32[]{:S(2)}) copy-start(bf16[16,4096]{1,0:T(8,128)(2,1)} %param.27) | copy-start | bytes 393220
  20.9 144.0 %all-gather.3.cloned.1.call-start = ((), (), s32[]{:S(2)}) async-start(), calls=%async_computation.2 | async-start | bytes 17571840 | tf_op jit(solution)/shard_map/all_gather | solution.py:529
  53.9 13.0 %copy-start.11 = (s32[1,8]{1,0:T(1,128)S(1)}, s32[1,8]{1,0:T(1,128)}, u32[]{:S(2)}) copy-start(s32[1,8]{1,0:T(1,128)} %param.29) | copy-start | bytes 100
  53.9 13.2 %copy-start.10 = (s32[1,512]{1,0:T(1,128)S(1)}, s32[1,512]{1,0:T(1,128)}, u32[]{:S(2)}) copy-start(s32[1,512]{1,0:T(1,128)} %param.28) | copy-start | bytes 6148
  53.9 13.3 %copy-start.8 = (s32[1280]{0:T(1024)S(1)}, s32[1280]{0:T(1024)}, u32[]{:S(2)}) copy-start(s32[1280]{0:T(1024)} %param.20) | copy-start | bytes 15364
  56.9 20.3 %all-to-all-start = ((bf16[64,2,512]{2,1,0:T(2,128)(2,1)}), bf16[64,2,512]{2,1,0:T(2,128)(2,1)S(1)}, u32[]{:S(2)}, u32[]{:S(2)}) async-start(bf16[64,2,512]{2,1,0:T(2,128)(2,1)} %reshape.631), calls=%async_computation | async-start | bytes 262144 | tf_op jit(solution)/shard_map/all_to_all | solution.py:538
  192.0 8.5 %copy-start.6 = (f32[4096]{0:T(1024)S(1)}, f32[4096]{0:T(1024)}, u32[]{:S(2)}) copy-start(f32[4096]{0:T(1024)} %param.31) | copy-start | bytes 49156
  192.0 9.1 %copy-start.7 = (f32[4096]{0:T(1024)S(1)}, f32[4096]{0:T(1024)}, u32[]{:S(2)}) copy-start(f32[4096]{0:T(1024)} %param.30) | copy-start | bytes 49156
  198.8 2.9 %collective-permute-start = (bf16[512,64]{1,0:T(8,128)(2,1)S(1)}, bf16[512,64]{1,0:T(8,128)(2,1)S(1)}, u32[]{:S(2)}, u32[]{:S(2)}) collective-permute-start(bf16[512,64]{1,0:T(8,128)(2,1)S(1)} %bitcast.84), channel_id=1, source_target_pairs={{0,1},{1,0},{2,3},{3,2},{4,5},{5,4},{6,7},{7,6},{8,9},{9,8},{10,11... | collective-permute-start | bytes 196616 | tf_op jit(solution)/shard_map/ppermute | solution.py:544
Sparse Core Ops, SparseCore 0:
  21.0 31.8 all-reduce.1
  56.2 108.6 all-gather.2
